TPU v7x, 32 devices: a whole 2x2x4 slice. The times are simulated.
32 devices in a mesh: dp: 4 (over y, core), tp: 8 (over z, x).
Axes of the slice: x: 2, y: 2, z: 4, core: 2. Of those that a mesh axis runs over, the one named last changes fastest.
Arguments:
- teacher_partial: bfloat16 [8, 512, 4608], P('tp', 'dp'), may hold values from -5 to 5
- teacher_residual: bfloat16 [512, 4608], P(('dp', 'tp')), may hold values from -120 to 120
- post_gain: float32 [4608], replicated, may hold values from 0.5 to 1.5
- final_gain: float32 [4608], replicated, may hold values from 0.5 to 1.5
- teacher_head: bfloat16 [4608, 32768], P(None, ('dp', 'tp')), may hold values from -40 to 40
- student_hidden: bfloat16 [512, 3584], P(('dp', 'tp')), may hold values from -120 to 120
- student_gain: float32 [3584], replicated, may hold values from 0.5 to 1.5
- student_head: bfloat16 [3584, 32768], P(None, ('dp', 'tp')), may hold values from -40 to 40
- labels: int32 [512], P('dp'), may hold values from 0 to 32767
- lengths: int32 [4, 8], P('dp'), may hold values from 1 to 48, 96 in all within a row
Outputs:
- grad_hidden: float32 [512, 3584], P(('dp', 'tp'))
- token_loss: float32 [512], P(('dp', 'tp'))
Inputs may be any that keep to these rules, and one draw needn't show every extreme that they name: `lengths`: group g's 8 sequences fill, in order, its first 96 rows; its remaining 128 - 96 rows are padding.
All inputs are finite; a program needn't handle non-finite values.
Results may differ from a plain program's by a relative error of at most 0.03.
Values may be sent and summed in bfloat16 or wider, within the bound.
No kernel may reach another device: no remote copies, remote signals or barrier semaphores. Data moves between devices by JAX's collectives and lax.ppermute only.
A program may use at most 128 MiB of HBM per device.

v0:
```python
import jax
import jax.numpy as jnp
from jax import lax
from jax.sharding import PartitionSpec as P

EPS = 1e-06
BETA = 0.5
LOSS_SCALE = 1024.0


def norm_rows(values, gain):
    inverse = lax.rsqrt(jnp.mean(values * values, axis=-1, keepdims=True) + EPS)
    return (values * inverse * gain, inverse)


def token_weights(lengths, tok_rows):
    ends = jnp.cumsum(lengths, axis=1)
    starts = ends - lengths
    places = jnp.arange(tok_rows, dtype=jnp.int32)
    inside = (places[None, :, None] >= starts[:, None, :]) & (
        places[None, :, None] < ends[:, None, :]
    )
    spans = jnp.sum(jnp.where(inside, lengths[:, None, :], 0), axis=2)
    covered = jnp.sum(inside.astype(jnp.int32), axis=2)
    return covered.astype(jnp.float32) / jnp.maximum(spans, 1).astype(jnp.float32)


def shards(
    teacher_partial,
    teacher_residual,
    post_gain,
    final_gain,
    teacher_head,
    student_hidden,
    student_gain,
    student_head,
    labels,
    lengths,
):
    share = teacher_residual.shape[0]
    tok_rows = labels.shape[0]
    mlp_sum = lax.psum_scatter(
        teacher_partial[0].astype(jnp.float32).astype(jnp.bfloat16),
        "tp",
        scatter_dimension=0,
        tiled=True,
    ).astype(jnp.float32)
    post, unused = norm_rows(mlp_sum, post_gain)
    final = teacher_residual.astype(jnp.float32) + post
    teacher_norm = norm_rows(final, final_gain)[0].astype(jnp.bfloat16)
    student_f = student_hidden.astype(jnp.float32)
    student_scaled, inverse = norm_rows(student_f, student_gain)
    student_norm = student_scaled.astype(jnp.bfloat16)
    label_all, length_all = (
        lax.all_gather(labels, "dp", axis=0, tiled=True),
        lax.all_gather(lengths, "dp", axis=0, tiled=True),
    )
    groups = length_all.shape[0]
    weight_all = token_weights(length_all, tok_rows)
    whole_t, whole_s = (
        lax.all_gather(teacher_norm, ("dp", "tp"), axis=0, tiled=True),
        lax.all_gather(student_norm, ("dp", "tp"), axis=0, tiled=True),
    )
    label_rows = label_all.reshape(groups, tok_rows).reshape(-1)
    weight_rows = weight_all.reshape(-1)
    vocab_dev = teacher_head.shape[1]
    position = lax.axis_index("dp") * lax.axis_size("tp") + lax.axis_index("tp")
    columns = position * vocab_dev + jnp.arange(vocab_dev, dtype=jnp.int32)
    t_logits = jnp.dot(whole_t, teacher_head, preferred_element_type=jnp.float32)
    s_logits = jnp.dot(whole_s, student_head, preferred_element_type=jnp.float32)
    hit = label_rows[:, None] == columns[None, :]
    label_logit = jnp.sum(jnp.where(hit, s_logits, 0.0), axis=1)
    t_local = jnp.max(t_logits, axis=1)
    s_local = jnp.max(s_logits, axis=1)
    t_max, s_max = lax.pmax((t_local, s_local), ("dp", "tp"))
    t_exp = jnp.exp(t_logits - t_max[:, None])
    s_exp = jnp.exp(s_logits - s_max[:, None])
    t_total, t_cross, s_total, label_value = lax.psum(
        (
            jnp.sum(t_exp, axis=1),
            jnp.sum(t_exp * (t_logits - s_logits), axis=1),
            jnp.sum(s_exp, axis=1),
            label_logit,
        ),
        ("dp", "tp"),
    )
    t_log = t_max + jnp.log(t_total)
    s_log = s_max + jnp.log(s_total)
    divergence = t_cross / t_total - t_log + s_log
    label_term = s_log - label_value
    row_loss = jnp.where(weight_rows > 0, divergence + BETA * label_term, 0.0)
    t_prob = t_exp / t_total[:, None]
    s_prob = s_exp / s_total[:, None]
    scale = (LOSS_SCALE * weight_rows)[:, None]
    logit_grad = (scale * ((1.0 + BETA) * s_prob - t_prob - BETA * hit.astype(jnp.float32))).astype(
        jnp.bfloat16
    )
    summed = lax.psum_scatter(
        lax.dot_general(
            logit_grad, student_head, (((1,), (1,)), ((), ())), preferred_element_type=jnp.float32
        ),
        ("dp", "tp"),
        scatter_dimension=0,
        tiled=True,
    )
    scaled = summed * student_gain
    inner = jnp.mean(scaled * student_f, axis=1, keepdims=True)
    grad_hidden = inverse * scaled - student_f * (inverse * inverse * inverse) * inner
    token_loss = lax.dynamic_slice_in_dim(row_loss, position * share, share, 0)
    return (grad_hidden, token_loss)


def solution(mesh):
    placed = (
        P("tp", "dp", None),
        P(("dp", "tp"), None),
        P(),
        P(),
        P(None, ("dp", "tp")),
        P(("dp", "tp"), None),
        P(),
        P(None, ("dp", "tp")),
        P("dp"),
        P("dp", None),
    )
    return jax.shard_map(
        shards,
        mesh=mesh,
        in_specs=placed,
        out_specs=(P(("dp", "tp"), None), P(("dp", "tp"))),
        check_vma=False,
    )
```

profile of v0, /device:TPU:0, one launch (start us, length us, event | category | flops | bytes accessed | tf_op | source)
XLA Modules:
  0.0 426.0 jit_solution(3692011497358117005)
XLA Ops:
  8.1 0.7 reduce-scatter.3.cloned.1.call-update
  8.8 1.0 fusion.21
  9.9 1.7 fusion.23
  11.6 0.0 all-gather.7.cloned.1.call-start
  11.6 70.1 %reduce-scatter.3.cloned.1.call-done = bf16[16,4608]{1,0:T(8,128)(2,1)} async-done(((bf16[128,4608]{1,0:T(8,128)(2,1)}), bf16[16,4608]{1,0:T(8,128)(2,1)}) %reduce-scatter.3.cloned.1.call-update) | async-done | bytes 147472 | tf_op jit(solution)/shard_map/reduce_scatter | solution.py:42
  81.7 1.1 fusion.18
  82.8 1.2 multiply_reduce_fusion.1
  84.0 1.7 multiply_convert_fusion
  85.8 0.0 reduce-scatter.5.cloned.1.call-start
  85.8 5.1 %all-gather = s32[4,1,8]{2,1,0:T(1,128)S(1)} all-gather(s32[1,1,8]{2,1,0:T(1,128)S(1)} %bitcast.20), channel_id=1, replica_groups=mesh['dp'=4,'tp'=8] {'dp'}, dimensions={0}, use_global_device_ids=true | all-gather | bytes 160 | tf_op jit(solution)/shard_map/all_gather | solution.py:56
  90.9 0.2 reduce_window_sum.11
  91.1 5.0 %all-gather.1 = s32[4,1,128]{2,1,0:T(1,128)S(1)} all-gather(s32[1,1,128]{2,1,0:T(1,128)S(1)} %bitcast.21), channel_id=1, replica_groups=mesh['dp'=4,'tp'=8] {'dp'}, dimensions={0}, use_global_device_ids=true | all-gather | bytes 2560 | tf_op jit(solution)/shard_map/all_gather | solution.py:55
  96.1 0.1 convert_reduce_fusion
  96.3 7.5 %fusion.32 = (f32[512]{0:T(512)S(1)}, f32[512,1024]{1,0:T(8,128)S(1)}) fusion(bf16[512,3584]{1,0:T(8,128)(2,1)} %all-gather.5.cloned.1.call-done, bf16[3584,1024]{1,0:T(8,128)(2,1)} %param.17), kind=kOutput, calls=%fused_computation.57 | convolution fusion | flops 3758620160 | bytes 13109248 | tf_op jit(solution)/shard_map/dot_general | solution.py:70
  103.8 45.2 %all-gather.7.cloned.1.call-done = bf16[512,4608]{1,0:T(8,128)(2,1)} async-done(((bf16[16,4608]{1,0:T(8,128)(2,1)}), bf16[512,4608]{1,0:T(8,128)(2,1)}) %all-gather.7.cloned.1.call-update) | async-done | bytes 4718608 | tf_op jit(solution)/shard_map/all_gather | solution.py:61
  149.0 10.1 %fusion.31 = (f32[512]{0:T(512)S(1)}, f32[512,1024]{1,0:T(8,128)}) fusion(bf16[512,4608]{1,0:T(8,128)(2,1)} %all-gather.7.cloned.1.call-done, bf16[4608,1024]{1,0:T(8,128)(2,1)} %param.14), kind=kOutput, calls=%fused_computation.56 | convolution fusion | flops 4832361984 | bytes 16254976 | tf_op jit(solution)/shard_map/dot_general | solution.py:69
  159.1 39.0 %all-reduce.1 = (f32[512]{0:T(512)S(1)}, f32[512]{0:T(512)S(1)}) all-reduce(f32[512]{0:T(512)S(1)} %get-tuple-element.16, f32[512]{0:T(512)S(1)} %get-tuple-element.18), channel_id=1, replica_groups=mesh['dp'=4,'tp'=8] {'dp','tp'}, use_global_device_ids=true, to_apply=%region_12.13 | all-reduce | flops 1024 | bytes 8192 | tf_op jit(solution)/shard_map/pmax | solution.py:75
  198.1 2.8 multiply_reduce_fusion
  200.9 40.1 %all-reduce = (f32[512]{0:T(512)S(1)}, f32[512]{0:T(512)S(1)}, f32[512]{0:T(512)S(1)}, f32[512]{0:T(512)S(1)}) all-reduce(f32[512]{0:T(512)S(1)} %get-tuple-element.3, f32[512]{0:T(512)S(1)} %get-tuple-element.5, f32[512]{0:T(512)S(1)} %get-tuple-element.4, f32[512]{0:T(512)S(1)} %get-tuple-element.2), channel_id=1, replica_groups=mesh['dp'=4,'tp'=8] {'dp','tp'}, use_global_device_ids=true, to_apply=%region_14.15 | all-reduce | flops 2048 | bytes 16384 | tf_op jit(solution)/shard_map/psum | solution.py:78
  241.0 11.6 %fusion.6 = f32[512,3584]{1,0:T(8,128)} fusion(bf16[3584,1024]{1,0:T(8,128)(2,1)} %param.17, f32[512,1024]{1,0:T(8,128)} %get-tuple-element.17, f32[512,1024]{1,0:T(8,128)S(1)} %get-tuple-element.19, s32[1024]{0:T(1024)S(1)} %iota_add_fusion, f32[512]{0:T(512)S(1)} %get-tuple-element.8, f32[512]{0:T(512)S(1)} %get-tuple-element.12, ...), kind=kOutput, calls=%fused_computation.11 | convolution fusion | flops 3763863552 | bytes 18890752 | tf_op jit(solution)/shard_map/dot_general | solution.py:99
  252.6 0.6 dynamic_slice.3
  253.2 162.3 %reduce-scatter.5.cloned.1.call-done = f32[16,3584]{1,0:T(8,128)} async-done(((f32[512,3584]{1,0:T(8,128)}), f32[16,3584]{1,0:T(8,128)}) %reduce-scatter.5.cloned.1.call-update) | async-done | bytes 229392 | tf_op jit(solution)/shard_map/reduce_scatter | solution.py:98
  415.5 1.1 fusion.26
  416.6 1.7 fusion.25
  (28 shorter events, 0.3 us)
Async XLA Ops:
  8.0 76.0 %copy-start.3 = (f32[4608]{0:T(1024)S(1)}, f32[4608]{0:T(1024)}, u32[]{:S(2)}) copy-start(f32[4608]{0:T(1024)} %param.12) | copy-start | bytes 55300
  8.0 76.0 %copy-start.1 = (bf16[16,4608]{1,0:T(8,128)(2,1)S(1)}, bf16[16,4608]{1,0:T(8,128)(2,1)}, u32[]{:S(2)}) copy-start(bf16[16,4608]{1,0:T(8,128)(2,1)} %param.11) | copy-start | bytes 442372
  8.0 76.0 %copy-start.4 = (f32[4608]{0:T(1024)S(1)}, f32[4608]{0:T(1024)}, u32[]{:S(2)}) copy-start(f32[4608]{0:T(1024)} %param.13) | copy-start | bytes 55300
  8.0 77.8 %copy-start.5 = (s32[1,8]{1,0:T(1,128)S(1)}, s32[1,8]{1,0:T(1,128)}, u32[]{:S(2)}) copy-start(s32[1,8]{1,0:T(1,128)} %param.19) | copy-start | bytes 100
  8.0 83.0 %copy-start.6 = (s32[128]{0:T(128)S(1)}, s32[128]{0:T(128)}, u32[]{:S(2)}) copy-start(s32[128]{0:T(128)} %param.18) | copy-start | bytes 1540
  8.1 73.6 %reduce-scatter.3.cloned.1.call-start = ((), (), s32[]{:S(2)}) async-start(), calls=%async_computation.3 | async-start | bytes 1327104 | tf_op jit(solution)/shard_map/reduce_scatter | solution.py:42
  8.8 87.5 %all-gather.5.cloned.1.call-start = ((), (), s32[]{:S(2)}) async-start(), calls=%async_computation.2 | async-start | bytes 3784704 | tf_op jit(solution)/shard_map/all_gather | solution.py:62
  11.6 137.4 %all-gather.7.cloned.1.call-start = ((), (), s32[]{:S(2)}) async-start(), calls=%async_computation.4 | async-start | bytes 4866048 | tf_op jit(solution)/shard_map/all_gather | solution.py:61
  85.8 329.8 %reduce-scatter.5.cloned.1.call-start = ((), (), s32[]{:S(2)}) async-start(), calls=%async_computation.5 | async-start | bytes 7569408 | tf_op jit(solution)/shard_map/reduce_scatter | solution.py:98
  252.6 162.9 %copy-start = (bf16[16,3584]{1,0:T(8,128)(2,1)S(1)}, bf16[16,3584]{1,0:T(8,128)(2,1)}, u32[]{:S(2)}) copy-start(bf16[16,3584]{1,0:T(8,128)(2,1)} %param.15) | copy-start | bytes 344068
  252.6 162.9 %copy-start.2 = (f32[3584]{0:T(1024)S(1)}, f32[3584]{0:T(1024)}, u32[]{:S(2)}) copy-start(f32[3584]{0:T(1024)} %param.16) | copy-start | bytes 43012
Sparse Core Ops, SparseCore 0:
  12.2 69.3 reduce-scatter.2
Sparse Core Ops, SparseCore 1:
  12.1 64.3 all-gather.4
  85.9 63.1 all-gather.6
  252.7 162.8 reduce-scatter.4
where the time goes:
time: 426 us
  waiting for transfers between devices  278 us (65%)
  blocking collectives  89.2 us (21%)
  matrix products  29.2 us (7%)
  between operations  15.8 us (4%)
  other arithmetic  12.6 us (3%)
    reduce_scatter x1, waiting for transfers between devices, shards(): lax.psum_scatter(lax.dot_general(logit_grad, student_head, (((1,), (1,)),...  162 us
    reduce_scatter x1, waiting for transfers between devices, shards(): lax.psum_scatter(teacher_partial[0].astype(jnp.float32).astype(jnp.bfloat...  70.1 us
    all_gather x1, waiting for transfers between devices, shards(): lax.all_gather(teacher_norm, ('dp', 'tp'), axis=0, tiled=True)  45.2 us
    psum x1, blocking collectives, shards(): lax.psum((jnp.sum(t_exp, axis=1), jnp.sum(t_exp * (t_logits - s_logits),...  40.1 us
    pmax x1, blocking collectives, shards(): t_max, s_max = lax.pmax((t_local, s_local), ('dp', 'tp'))  39 us
    dot_general x1, matrix products, shards(): lax.dot_general(logit_grad, student_head, (((1,), (1,)), ((), ())), prefe...  11.6 us
    dot_general x1, matrix products, shards(): jnp.dot(whole_t, teacher_head, preferred_element_type=jnp.float32)  10.1 us
  transfers between devices with their start and end apart: 4, of which 3 were waited for; matrix products, arithmetic and copies ran while one was open for 4% of the time, Pallas kernels for 0%

commit v1 on v0

--- a/solution.py
+++ b/solution.py
@@ -76,13 +76,16 @@
     t_exp = jnp.exp(t_logits - t_max[:, None])
     s_exp = jnp.exp(s_logits - s_max[:, None])
     t_total, t_cross, s_total, label_value = lax.psum(
-        (
-            jnp.sum(t_exp, axis=1),
-            jnp.sum(t_exp * (t_logits - s_logits), axis=1),
-            jnp.sum(s_exp, axis=1),
-            label_logit,
+        lax.psum(
+            (
+                jnp.sum(t_exp, axis=1),
+                jnp.sum(t_exp * (t_logits - s_logits), axis=1),
+                jnp.sum(s_exp, axis=1),
+                label_logit,
+            ),
+            "tp",
         ),
-        ("dp", "tp"),
+        "dp",
     )
     t_log = t_max + jnp.log(t_total)
     s_log = s_max + jnp.log(s_total)

time: 426 us -> 412 us (0.967)
  blocking collectives: 89.2 us -> 75.6 us
    psum x1, blocking collectives: 40.1 us -> 20.8 us  [shards(): lax.psum((jnp.sum(t_exp, axis=1), jnp.sum(t_exp * (t_logits - s_logits),...]
    psum x0 -> x1, blocking collectives: none -> 5.74 us  [shards(): lax.psum(lax.psum((jnp.sum(t_exp, axis=1), jnp.sum(t_exp * (t_logits - s_...]
where the time goes in v1:
time: 412 us; the launch traced here: 410 us
  waiting for transfers between devices  276 us (67%)
  blocking collectives  75.6 us (18%)
  matrix products  29.2 us (7%)
  between operations  15.8 us (4%)
  other arithmetic  12.6 us (3%)
    reduce_scatter x1, waiting for transfers between devices, shards(): lax.psum_scatter(lax.dot_general(logit_grad, student_head, (((1,), (1,)),...  160 us
    reduce_scatter x1, waiting for transfers between devices, shards(): lax.psum_scatter(teacher_partial[0].astype(jnp.float32).astype(jnp.bfloat...  70.1 us
    all_gather x1, waiting for transfers between devices, shards(): lax.all_gather(teacher_norm, ('dp', 'tp'), axis=0, tiled=True)  45.2 us
    pmax x1, blocking collectives, shards(): t_max, s_max = lax.pmax((t_local, s_local), ('dp', 'tp'))  39 us
    psum x1, blocking collectives, shards(): lax.psum((jnp.sum(t_exp, axis=1), jnp.sum(t_exp * (t_logits - s_logits),...  20.8 us
    dot_general x1, matrix products, shards(): lax.dot_general(logit_grad, student_head, (((1,), (1,)), ((), ())), prefe...  11.6 us
    dot_general x1, matrix products, shards(): jnp.dot(whole_t, teacher_head, preferred_element_type=jnp.float32)  10.1 us
  transfers between devices with their start and end apart: 4, of which 3 were waited for; matrix products, arithmetic and copies ran while one was open for 4% of the time, Pallas kernels for 0%

profile of v1, /device:TPU:0, one launch (start us, length us, event | category | flops | bytes accessed | tf_op | source)
XLA Modules:
  0.0 410.5 jit_solution(9961711488785132773)
XLA Ops:
  8.1 0.7 reduce-scatter.3.cloned.1.call-update
  8.8 1.0 fusion.21
  9.9 1.7 fusion.23
  11.6 0.0 all-gather.7.cloned.1.call-start
  11.6 70.1 %reduce-scatter.3.cloned.1.call-done = bf16[16,4608]{1,0:T(8,128)(2,1)} async-done(((bf16[128,4608]{1,0:T(8,128)(2,1)}), bf16[16,4608]{1,0:T(8,128)(2,1)}) %reduce-scatter.3.cloned.1.call-update) | async-done | bytes 147472 | tf_op jit(solution)/shard_map/reduce_scatter | solution.py:42
  81.7 1.1 fusion.18
  82.8 1.2 multiply_reduce_fusion.1
  84.0 1.7 multiply_convert_fusion
  85.8 5.1 %all-gather = s32[4,1,8]{2,1,0:T(1,128)S(1)} all-gather(s32[1,1,8]{2,1,0:T(1,128)S(1)} %bitcast.20), channel_id=1, replica_groups=mesh['dp'=4,'tp'=8] {'dp'}, dimensions={0}, use_global_device_ids=true | all-gather | bytes 160 | tf_op jit(solution)/shard_map/all_gather | solution.py:56
  90.9 0.2 reduce_window_sum.11
  91.1 5.0 %all-gather.1 = s32[4,1,128]{2,1,0:T(1,128)S(1)} all-gather(s32[1,1,128]{2,1,0:T(1,128)S(1)} %bitcast.21), channel_id=1, replica_groups=mesh['dp'=4,'tp'=8] {'dp'}, dimensions={0}, use_global_device_ids=true | all-gather | bytes 2560 | tf_op jit(solution)/shard_map/all_gather | solution.py:55
  96.1 0.1 convert_reduce_fusion
  96.3 7.5 %fusion.32 = (f32[512]{0:T(512)S(1)}, f32[512,1024]{1,0:T(8,128)S(1)}) fusion(bf16[512,3584]{1,0:T(8,128)(2,1)} %all-gather.5.cloned.1.call-done, bf16[3584,1024]{1,0:T(8,128)(2,1)} %param.17), kind=kOutput, calls=%fused_computation.57 | convolution fusion | flops 3758620160 | bytes 13109248 | tf_op jit(solution)/shard_map/dot_general | solution.py:70
  103.8 45.2 %all-gather.7.cloned.1.call-done = bf16[512,4608]{1,0:T(8,128)(2,1)} async-done(((bf16[16,4608]{1,0:T(8,128)(2,1)}), bf16[512,4608]{1,0:T(8,128)(2,1)}) %all-gather.7.cloned.1.call-update) | async-done | bytes 4718608 | tf_op jit(solution)/shard_map/all_gather | solution.py:61
  149.0 10.1 %fusion.31 = (f32[512]{0:T(512)S(1)}, f32[512,1024]{1,0:T(8,128)}) fusion(bf16[512,4608]{1,0:T(8,128)(2,1)} %all-gather.7.cloned.1.call-done, bf16[4608,1024]{1,0:T(8,128)(2,1)} %param.14), kind=kOutput, calls=%fused_computation.56 | convolution fusion | flops 4832361984 | bytes 16254976 | tf_op jit(solution)/shard_map/dot_general | solution.py:69
  159.1 39.0 %all-reduce = (f32[512]{0:T(512)S(1)}, f32[512]{0:T(512)S(1)}) all-reduce(f32[512]{0:T(512)S(1)} %get-tuple-element.20, f32[512]{0:T(512)S(1)} %get-tuple-element.22), channel_id=1, replica_groups=mesh['dp'=4,'tp'=8] {'dp','tp'}, use_global_device_ids=true, to_apply=%region_13.14 | all-reduce | flops 1024 | bytes 8192 | tf_op jit(solution)/shard_map/pmax | solution.py:75
  198.1 2.8 multiply_reduce_fusion
  200.9 20.8 %all-reduce.1 = (f32[512]{0:T(512)S(1)}, f32[512]{0:T(512)S(1)}, f32[512]{0:T(512)S(1)}, f32[512]{0:T(512)S(1)}) all-reduce(f32[512]{0:T(512)S(1)} %get-tuple-element.3, f32[512]{0:T(512)S(1)} %get-tuple-element.5, f32[512]{0:T(512)S(1)} %get-tuple-element.4, f32[512]{0:T(512)S(1)} %get-tuple-element.2), channel_id=1, replica_groups=mesh['dp'=4,'tp'=8] {'tp'}, use_global_device_ids=true, to_apply=%region_15.16 | all-reduce | flops 2048 | bytes 16384 | tf_op jit(solution)/shard_map/psum | solution.py:79
  221.7 5.7 %all-reduce.2 = (f32[512]{0:T(512)S(1)}, f32[512]{0:T(512)S(1)}, f32[512]{0:T(512)S(1)}, f32[512]{0:T(512)S(1)}) all-reduce(f32[512]{0:T(512)S(1)} %get-tuple-element.10, f32[512]{0:T(512)S(1)} %get-tuple-element.11, f32[512]{0:T(512)S(1)} %get-tuple-element.12, f32[512]{0:T(512)S(1)} %get-tuple-element.13), channel_id=1, replica_groups=mesh['dp'=4,'tp'=8] {'dp'}, use_global_device_ids=true, to_apply=%region_16.17 | all-reduce | flops 2048 | bytes 16384 | tf_op jit(solution)/shard_map/psum | solution.py:78
  227.4 11.6 %fusion.6 = f32[512,3584]{1,0:T(8,128)} fusion(bf16[3584,1024]{1,0:T(8,128)(2,1)} %param.17, f32[512,1024]{1,0:T(8,128)} %get-tuple-element.21, f32[512,1024]{1,0:T(8,128)S(1)} %get-tuple-element.23, s32[1024]{0:T(1024)S(1)} %iota_add_fusion, f32[512]{0:T(512)S(1)} %get-tuple-element.14, f32[512]{0:T(512)S(1)} %get-tuple-element.8, ...), kind=kOutput, calls=%fused_computation.11 | convolution fusion | flops 3763863552 | bytes 18890752 | tf_op jit(solution)/shard_map/dot_general | solution.py:102
  239.1 0.6 dynamic_slice.3
  239.7 160.4 %reduce-scatter.5.cloned.1.call-done = f32[16,3584]{1,0:T(8,128)} async-done(((f32[512,3584]{1,0:T(8,128)}), f32[16,3584]{1,0:T(8,128)}) %reduce-scatter.5.cloned.1.call-update) | async-done | bytes 229392 | tf_op jit(solution)/shard_map/reduce_scatter | solution.py:101
  400.0 1.1 fusion.26
  401.1 1.7 fusion.25
  (29 shorter events, 0.3 us)
Async XLA Ops:
  8.0 76.0 %copy-start.3 = (f32[4608]{0:T(1024)S(1)}, f32[4608]{0:T(1024)}, u32[]{:S(2)}) copy-start(f32[4608]{0:T(1024)} %param.12) | copy-start | bytes 55300
  8.0 76.0 %copy-start.1 = (bf16[16,4608]{1,0:T(8,128)(2,1)S(1)}, bf16[16,4608]{1,0:T(8,128)(2,1)}, u32[]{:S(2)}) copy-start(bf16[16,4608]{1,0:T(8,128)(2,1)} %param.11) | copy-start | bytes 442372
  8.0 76.0 %copy-start.4 = (f32[4608]{0:T(1024)S(1)}, f32[4608]{0:T(1024)}, u32[]{:S(2)}) copy-start(f32[4608]{0:T(1024)} %param.13) | copy-start | bytes 55300
  8.0 77.8 %copy-start.5 = (s32[1,8]{1,0:T(1,128)S(1)}, s32[1,8]{1,0:T(1,128)}, u32[]{:S(2)}) copy-start(s32[1,8]{1,0:T(1,128)} %param.19) | copy-start | bytes 100
  8.0 83.0 %copy-start.6 = (s32[128]{0:T(128)S(1)}, s32[128]{0:T(128)}, u32[]{:S(2)}) copy-start(s32[128]{0:T(128)} %param.18) | copy-start | bytes 1540
  8.1 73.6 %reduce-scatter.3.cloned.1.call-start = ((), (), s32[]{:S(2)}) async-start(), calls=%async_computation.3 | async-start | bytes 1327104 | tf_op jit(solution)/shard_map/reduce_scatter | solution.py:42
  8.8 87.5 %all-gather.5.cloned.1.call-start = ((), (), s32[]{:S(2)}) async-start(), calls=%async_computation.2 | async-start | bytes 3784704 | tf_op jit(solution)/shard_map/all_gather | solution.py:62
  11.6 137.4 %all-gather.7.cloned.1.call-start = ((), (), s32[]{:S(2)}) async-start(), calls=%async_computation.4 | async-start | bytes 4866048 | tf_op jit(solution)/shard_map/all_gather | solution.py:61
  85.8 314.3 %reduce-scatter.5.cloned.1.call-start = ((), (), s32[]{:S(2)}) async-start(), calls=%async_computation.5 | async-start | bytes 7569408 | tf_op jit(solution)/shard_map/reduce_scatter | solution.py:101
  239.0 161.0 %copy-start = (bf16[16,3584]{1,0:T(8,128)(2,1)S(1)}, bf16[16,3584]{1,0:T(8,128)(2,1)}, u32[]{:S(2)}) copy-start(bf16[16,3584]{1,0:T(8,128)(2,1)} %param.15) | copy-start | bytes 344068
  239.0 161.0 %copy-start.2 = (f32[3584]{0:T(1024)S(1)}, f32[3584]{0:T(1024)}, u32[]{:S(2)}) copy-start(f32[3584]{0:T(1024)} %param.16) | copy-start | bytes 43012
Sparse Core Ops, SparseCore 0:
  12.2 69.3 reduce-scatter.2
Sparse Core Ops, SparseCore 1:
  12.1 64.3 all-gather.4
  85.9 63.1 all-gather.6
  239.1 160.8 reduce-scatter.4
